TPU v7x, 32 devices: a whole 2x2x4 slice. The times are simulated.
32 devices in a mesh: head: 2 (over x), expert: 16 (over z, y, core).
Axes of the slice: x: 2, y: 2, z: 4, core: 2. Of those that a mesh axis runs over, the one named last changes fastest.
Arguments:
- queries: bfloat16 [256, 128, 576], P('expert', 'head'), may hold values from -64 to 64
- resident_cache: bfloat16 [64, 256, 576], P('expert'), may hold values from -6 to 6
- resident_len: int32 [64], P('expert'), may hold values from 1 to 256, as said below
- new_cache: bfloat16 [192, 64, 576], P('expert'), may hold values from -6 to 6
- new_len: int32 [192], replicated, may hold values from 1 to 64, as said below
- new_owner: int32 [192], replicated, may hold values from 0 to 15, as said below
- value_up: bfloat16 [128, 512, 128], P('head'), may hold values from -0.25 to 0.25
- w_output: bfloat16 [16384, 7168], P('head', 'expert'), may hold values from -0.046875 to 0.046875
- residual: bfloat16 [256, 7168], P(None, 'expert'), may hold values from -6 to 6
- expert_ids: int32 [256, 8], replicated, may hold values from 0 to 15, all different within a row; in each aligned block of 16 rows (0 to 15, 16 to 31, ...) at most 12 rows name the same one
- expert_gates: float32 [256, 8], replicated, may hold values from 0.1 to 1
- norm_gain: bfloat16 [7168], replicated, may hold values from 0.5 to 1.5
- w_gate: bfloat16 [16, 7168, 1024], P('expert', None, 'head'), may hold values from -0.0625 to 0.0625
- w_up: bfloat16 [16, 7168, 1024], P('expert', None, 'head'), may hold values from -0.0625 to 0.0625
- w_down: bfloat16 [16, 1024, 7168], P('expert', 'head'), may hold values from -0.1875 to 0.1875
Outputs:
- layer_out: bfloat16 [256, 7168], P('head', 'expert')
Inputs may be any that keep to these rules, and one draw needn't show every extreme that they name: `resident_len`: every decode owner has a resident request of length 256. `new_len`: every prefill device holds a new request of length 64. `new_owner`: one prefill device sends at most 2 of its 12 new requests to one decode owner, and every decode owner receives exactly 12 in all; a prefill device sends either 2 or none to each owner, except to at most one owner, which gets the remainder of 12 divided by 2. `expert_ids`: in each aligned block of 16 rows (the rows of one decode owner) no expert is named by more than 12 rows; the 8 experts of a row differ.
All inputs are finite; a program needn't handle non-finite values.
Results may differ from a plain program's by a relative error of at most 0.012.
Values may be sent and summed in bfloat16 or wider, within the bound.
A program may use at most 128 MiB of HBM per device.

v0:
```python
import jax
import jax.numpy as jnp
from jax import lax
from jax.sharding import PartitionSpec as P

ROPE = 64
NOPE = 128


def attend(queries, caches, length, value_up):
    inverse_root = (NOPE + ROPE) ** (-0.5)
    latent_width = value_up.shape[1]
    scores = (
        jnp.einsum("rhc,rtc->rht", queries, caches, preferred_element_type=jnp.float32)
        * inverse_root
    )
    inside = lax.broadcasted_iota(jnp.int32, scores.shape, 2) < length[:, None, None]
    scores = jnp.where(inside, scores, -jnp.inf)
    highest = jnp.max(scores, axis=2, keepdims=True)
    raised = jnp.exp(scores - highest)
    weights = (raised / jnp.sum(raised, axis=2, keepdims=True)).astype(jnp.bfloat16)
    latent = jnp.einsum(
        "rht,rtc->rhc", weights, caches[:, :, :latent_width], preferred_element_type=jnp.float32
    ).astype(jnp.bfloat16)
    values = jnp.einsum(
        "rhc,hcv->rhv", latent, value_up, preferred_element_type=jnp.float32
    ).astype(jnp.bfloat16)
    return values.reshape(values.shape[0], -1)


def earlier_equal(labels):
    count = labels.shape[0]
    position = jnp.arange(count, dtype=jnp.int32)
    before = (labels[:, None] == labels[None, :]) & (position[None, :] < position[:, None])
    return jnp.sum(before.astype(jnp.int32), axis=1)


def per_device(
    queries,
    resident_cache,
    resident_len,
    new_cache,
    new_len,
    new_owner,
    value_up,
    w_output,
    residual,
    expert_ids,
    expert_gates,
    norm_gain,
    w_gate,
    w_up,
    w_down,
):
    n_expert = lax.axis_size("expert")
    n_head = lax.axis_size("head")
    owner_index = lax.axis_index("expert")
    head_index = lax.axis_index("head")
    req_count = resident_cache.shape[0]
    new_count = new_cache.shape[0]
    rows_dev = req_count + new_count
    rows_all = rows_dev * n_expert
    choose = expert_ids.shape[1]
    local_experts = w_gate.shape[0]
    experts = local_experts * n_expert
    column_slab = residual.shape[1]
    most = max(2, (4 * new_count + 3 * n_expert - 1) // (3 * n_expert))
    capacity = max(2, 3 * rows_dev * choose // (2 * experts))
    slots_all = n_expert * capacity
    group = n_expert // n_head
    block_rows = group * rows_dev
    cache_shape = new_cache.shape[1:]
    targets = lax.dynamic_slice_in_dim(new_owner, owner_index * new_count, new_count)
    places = targets * most + earlier_equal(targets)
    senders = (
        jnp.full((n_expert * most,), new_count, jnp.int32)
        .at[places]
        .set(jnp.arange(new_count, dtype=jnp.int32))
    )
    outgoing = jnp.take(new_cache, senders, axis=0, mode="fill", fill_value=0).reshape(
        (n_expert, most) + cache_shape
    )
    incoming = lax.all_to_all(outgoing, "expert", split_axis=0, concat_axis=0, tiled=True)
    ordering = jnp.argsort(new_owner, stable=True)
    chosen = lax.dynamic_slice_in_dim(ordering, owner_index * new_count, new_count)
    anchor = chosen // new_count
    arrived = jnp.take(
        incoming.reshape((n_expert * most,) + cache_shape),
        anchor * most + earlier_equal(anchor),
        axis=0,
    )
    resident_att = attend(queries[:req_count], resident_cache, resident_len, value_up)
    arrived_att = attend(queries[req_count:], arrived, new_len[chosen], value_up)
    attention = jnp.concatenate([resident_att, arrived_att], axis=0)
    mixed = jnp.dot(
        lax.all_gather(attention, "expert", axis=0, tiled=True),
        w_output,
        preferred_element_type=jnp.float32,
    )
    picks = expert_ids.reshape(n_expert, rows_dev * choose)
    onehot = (picks[:, :, None] == jnp.arange(experts, dtype=jnp.int32)[None, None, :]).astype(
        jnp.int32
    )
    ranking = jnp.sum(jnp.cumsum(onehot, axis=1) * onehot, axis=2) - 1
    source = jnp.broadcast_to(jnp.arange(n_expert, dtype=jnp.int32)[:, None], picks.shape)
    slot_index = picks * slots_all + source * capacity + ranking
    row_index = (
        source * rows_dev + jnp.arange(rows_dev * choose, dtype=jnp.int32)[None, :] // choose
    )
    slot_rows = (
        jnp.full((experts * slots_all,), rows_all, jnp.int32)
        .at[slot_index.reshape(-1)]
        .set(row_index.reshape(-1))
    )
    summed = lax.psum(mixed, "head")
    hidden_all = (residual.astype(jnp.float32) + summed).astype(jnp.bfloat16)
    hidden_block = lax.dynamic_slice_in_dim(hidden_all, head_index * block_rows, block_rows)
    gathered = jnp.take(hidden_all, slot_rows, axis=0, mode="fill", fill_value=0).reshape(
        n_expert, local_experts * slots_all, column_slab
    )
    arrived_rows = lax.all_to_all(gathered, "expert", split_axis=0, concat_axis=2, tiled=True)
    inputs = arrived_rows.astype(jnp.float32)
    inverse = lax.rsqrt(jnp.mean(inputs * inputs, axis=2, keepdims=True) + 1e-06)
    normed = (inputs * inverse * norm_gain.astype(jnp.float32)).astype(jnp.bfloat16)
    gate_act = jnp.einsum("esd,edf->esf", normed, w_gate, preferred_element_type=jnp.float32)
    up_act = jnp.einsum("esd,edf->esf", normed, w_up, preferred_element_type=jnp.float32)
    hidden_act = (jax.nn.silu(gate_act) * up_act).astype(jnp.bfloat16)
    partial_value = jnp.einsum(
        "esf,efd->esd", hidden_act, w_down, preferred_element_type=jnp.float32
    )
    shared = lax.psum_scatter(
        partial_value.astype(jnp.bfloat16), "head", scatter_dimension=1, tiled=True
    ).astype(jnp.float32)
    returned = lax.all_to_all(
        shared.astype(jnp.bfloat16), "expert", split_axis=2, concat_axis=0, tiled=True
    ).astype(shared.dtype)
    ids_block = lax.dynamic_slice_in_dim(expert_ids, head_index * block_rows, block_rows)
    gates_block = lax.dynamic_slice_in_dim(expert_gates, head_index * block_rows, block_rows)
    source_block = (
        lax.dynamic_slice_in_dim(
            source.reshape(rows_all, choose), head_index * block_rows, block_rows
        )
        - head_index * group
    )
    rank_block = lax.dynamic_slice_in_dim(
        ranking.reshape(rows_all, choose), head_index * block_rows, block_rows
    )
    local_slot = ids_block * (group * capacity) + source_block * capacity + rank_block
    picked = jnp.take(
        returned.reshape(experts * group * capacity, column_slab), local_slot.reshape(-1), axis=0
    ).reshape(block_rows, choose, column_slab)
    routed_block = jnp.sum(picked * gates_block[:, :, None], axis=1)
    return (hidden_block.astype(jnp.float32) + routed_block).astype(jnp.bfloat16)


def solution(mesh):
    return jax.shard_map(
        per_device,
        mesh=mesh,
        in_specs=(
            P("expert", "head", None),
            P("expert", None, None),
            P("expert"),
            P("expert", None, None),
            P(),
            P(),
            P("head", None, None),
            P("head", "expert"),
            P(None, "expert"),
            P(),
            P(),
            P(),
            P("expert", None, "head"),
            P("expert", None, "head"),
            P("expert", "head", None),
        ),
        out_specs=P("head", "expert"),
        check_vma=False,
    )
```

profile of v0, /device:TPU:13, one launch (start us, length us, event | category | flops | bytes accessed | tf_op | source)
XLA Modules:
  0.0 468.8 jit_solution(2501718633419591748)
XLA Ops:
  7.6 3.8 sort.17
  15.3 3.5 broadcast_select_fusion.1
  18.9 6.7 %all-to-all-start = ((bf16[16,2,64,576]{3,2,1,0:T(8,128)(2,1)}), bf16[16,2,64,576]{3,2,1,0:T(8,128)(2,1)}, u32[]{:S(2)}, u32[]{:S(2)}) async-start(bf16[16,2,64,576]{3,2,1,0:T(8,128)(2,1)} %broadcast_select_fusion.1), calls=%async_computation | async-start | bytes 5242880 | tf_op jit(solution)/shard_map/all_to_all | solution.py:83
  30.1 4.6 fusion.28
  34.7 49.6 %all-to-all-done = bf16[16,2,64,576]{3,2,1,0:T(8,128)(2,1)} async-done(((bf16[16,2,64,576]{3,2,1,0:T(8,128)(2,1)}), bf16[16,2,64,576]{3,2,1,0:T(8,128)(2,1)}, u32[]{:S(2)}, u32[]{:S(2)}) %all-to-all-start) | async-done | bytes 2359328 | tf_op jit(solution)/shard_map/all_to_all | solution.py:83
  84.3 2.5 gather_fusion.2
  89.8 4.8 %fusion.26 = bf16[12,64,128]{2,0,1:T(8,128)(2,1)S(1)} fusion(bf16[64,512,128]{2,1,0:T(8,128)(2,1)} %param.21, bf16[12,64,512]{2,1,0:T(8,128)(2,1)S(1)} %convolution_convert_fusion.1), kind=kOutput, calls=%fused_computation.39 | convolution fusion | flops 100761600 | bytes 9371648 | tf_op jit(solution)/shard_map/rhc,hcv->rhv/dot_general | solution.py:25
  96.3 2.8 select_reduce_fusion
  99.6 45.6 %all-gather.2.cloned.1.call-done = bf16[256,8192]{1,0:T(8,128)(2,1)} async-done(((bf16[16,8192]{1,0:T(8,128)(2,1)}), bf16[256,8192]{1,0:T(8,128)(2,1)}) %all-gather.2.cloned.1.call-update) | async-done | bytes 4194320 | tf_op jit(solution)/shard_map/all_gather | solution.py:96
  145.2 7.2 %fusion.59 = f32[256,448]{0,1:T(8,128)} fusion(bf16[256,8192]{1,0:T(8,128)(2,1)} %all-gather.2.cloned.1.call-done, bf16[8192,448]{0,1:T(8,128)(2,1)} %param.22), kind=kOutput, calls=%fused_computation.117 | convolution fusion | flops 1879048192 | bytes 11993088 | tf_op jit(solution)/shard_map/dot_general | solution.py:95
  152.5 8.1 %scatter_custom_fusion.1 = s32[3072]{0:T(1024)S(1)} fusion(s32[2048]{0:T(1024)S(1)} %bitcast.83, s32[2048]{0:T(1024)S(1)} %add_bitcast_fusion, s32[]{:T(128)} %constant.124.clone.1), kind=kCustom, calls=%fused_computation.82 | custom fusion | bytes 12292 | tf_op jit(solution)/shard_map/scatter | solution.py:113
  160.7 18.0 %all-reduce.2.cloned.1.call-done = f32[256,448]{0,1:T(8,128)} async-done(((f32[256,448]{0,1:T(8,128)}), f32[256,448]{0,1:T(8,128)}) %all-reduce.2.cloned.1.call-update) | async-done | bytes 458768 | tf_op jit(solution)/shard_map/psum | solution.py:115
  179.9 13.2 %gather_fusion.3 = bf16[3072,448]{1,0:T(8,128)(2,1)} fusion(bf16[256,448]{1,0:T(8,128)(2,1)S(1)} %copy.104, s32[3072]{0:T(1024)S(1)} %fusion.47), kind=kCustom, calls=%fused_computation.3 | custom fusion | bytes 5517312 | tf_op jit(solution)/shard_map/jit(_take)/gather | solution.py:118
  193.1 3.4 broadcast_select_fusion
  196.5 6.6 %all-to-all-start.1 = ((bf16[16,192,448]{2,1,0:T(8,128)(2,1)}), bf16[16,192,448]{2,1,0:T(8,128)(2,1)}, u32[]{:S(2)}, u32[]{:S(2)}) async-start(bf16[16,192,448]{2,1,0:T(8,128)(2,1)} %broadcast_select_fusion), calls=%async_computation.1 | async-start | bytes 6291456 | tf_op jit(solution)/shard_map/all_to_all | solution.py:121
  203.2 69.9 %all-to-all-done.1 = bf16[16,192,448]{2,1,0:T(8,128)(2,1)} async-done(((bf16[16,192,448]{2,1,0:T(8,128)(2,1)}), bf16[16,192,448]{2,1,0:T(8,128)(2,1)}, u32[]{:S(2)}, u32[]{:S(2)}) %all-to-all-start.1) | async-done | bytes 2752544 | tf_op jit(solution)/shard_map/all_to_all | solution.py:121
  273.1 2.7 fusion.8
  275.8 2.8 fusion.11
  278.5 3.4 copy.105
  282.0 6.4 %convert_element_type.122 = bf16[192,7168]{1,0:T(8,128)(2,1)} reshape(bf16[1,192,16,448]{3,2,1,0:T(8,128)(2,1)} %copy.105) | data formatting | bytes 5505024 | tf_op jit(solution)/shard_map/convert_element_type | solution.py:124
  288.3 5.5 %fusion.6 = f32[192,512]{1,0:T(8,128)S(1)} fusion(bf16[192,7168]{1,0:T(8,128)(2,1)} %convert_element_type.122, bf16[1,7168,512]{2,1,0:T(8,128)(2,1)} %param.27), kind=kOutput, calls=%fused_computation.16 | convolution fusion | flops 1409286144 | bytes 10485760 | tf_op jit(solution)/shard_map/esd,edf->esf/dot_general | solution.py:125
  293.9 10.7 %fusion.2 = bf16[1,192,7168]{2,1,0:T(8,128)(2,1)} fusion(bf16[1,512,7168]{2,1,0:T(8,128)(2,1)} %param.29, bf16[192,7168]{1,0:T(8,128)(2,1)} %convert_element_type.122, bf16[1,7168,512]{2,1,0:T(8,128)(2,1)} %param.28, f32[192,512]{1,0:T(8,128)S(1)} %fusion.6), kind=kOutput, calls=%fused_computation.10 | convolution fusion | flops 2820538368 | bytes 20578304 | tf_op jit(solution)/shard_map/esf,efd->esd/dot_general | solution.py:128
  304.5 37.6 %reduce-scatter.2.cloned.1.call-done = bf16[1,96,7168]{2,1,0:T(8,128)(2,1)} async-done(((bf16[1,192,7168]{2,1,0:T(8,128)(2,1)}), bf16[1,96,7168]{2,1,0:T(8,128)(2,1)}) %reduce-scatter.2.cloned.1.call-update) | async-done | bytes 1376272 | tf_op jit(solution)/shard_map/reduce_scatter | solution.py:131
  342.1 8.5 %copy.106 = bf16[1,96,7168]{1,0,2:T(2,128)(2,1)} copy(bf16[1,96,7168]{2,1,0:T(8,128)(2,1)} %reduce-scatter.2.cloned.1.call-done) | data formatting | bytes 2752512 | tf_op jit(solution)/shard_map/reduce_scatter | solution.py:131
  351.1 39.8 %reduce.3 = bf16[7168,96]{1,0:T(8,128)(2,1)S(1)} reduce(bf16[7168,1,96]{2,1,0:T(2,128)(2,1)} %bitcast.74, bf16[]{:T(256)} %broadcast.267), dimensions={1}, to_apply=%bitcast.57.reduce_sub_computation | reduce | bytes 2752514
  390.9 3.9 reshape.370
  394.8 6.5 %all-to-all-start.2 = ((bf16[16,2,21504]{2,1,0:T(2,128)(2,1)}), bf16[16,2,21504]{2,1,0:T(2,128)(2,1)S(1)}, u32[]{:S(2)}, u32[]{:S(2)}) async-start(bf16[16,2,21504]{2,1,0:T(2,128)(2,1)} %reshape.370), calls=%async_computation.3 | async-start | bytes 2752512 | tf_op jit(solution)/shard_map/all_to_all | solution.py:134
  402.1 31.1 %all-to-all-done.2 = bf16[16,2,21504]{2,1,0:T(2,128)(2,1)S(1)} async-done(((bf16[16,2,21504]{2,1,0:T(2,128)(2,1)}), bf16[16,2,21504]{2,1,0:T(2,128)(2,1)S(1)}, u32[]{:S(2)}, u32[]{:S(2)}) %all-to-all-start.2) | async-done | bytes 1376288 | tf_op jit(solution)/shard_map/all_to_all | solution.py:134
  433.2 7.1 %reshape.371 = bf16[7168,1,96]{2,1,0:T(2,128)(2,1)} reshape(bf16[16,2,21504]{2,1,0:T(2,128)(2,1)S(1)} %all-to-all-done.2) | data formatting | bytes 2752512
  440.3 7.7 %bitcast_convert_fusion = f32[1,96,7168]{1,0,2:T(1,128)} fusion(bf16[7168,1,96]{2,1,0:T(2,128)(2,1)} %reshape.371), kind=kLoop, calls=%fused_computation.116 | loop fusion | flops 688128 | bytes 4128768 | tf_op jit(solution)/shard_map/convert_element_type | solution.py:136
  448.1 5.0 %copy.107 = f32[1,96,16,448]{3,1,2,0:T(8,128)} copy(f32[1,96,16,448]{1,3,2,0:T(8,128)} %bitcast.75) | data formatting | bytes 5505024 | tf_op jit(solution)/shard_map/convert_element_type | solution.py:136
  453.1 6.0 %gather_fusion.4 = f32[1024,448]{1,0:T(8,128)S(1)} fusion(f32[1536,448]{1,0:T(8,128)} %bitcast.73, s32[1024]{0:T(1024)S(1)} %broadcast_clamp_fusion), kind=kCustom, calls=%fused_computation.4 | custom fusion | bytes 3674112 | tf_op jit(solution)/shard_map/jit(_take)/gather | solution.py:149
  (92 shorter events, 20.5 us)
Async XLA Ops:
  6.5 6.4 %copy-start = (bf16[12,64,576]{2,1,0:T(8,128)(2,1)S(1)}, bf16[12,64,576]{2,1,0:T(8,128)(2,1)}, u32[]{:S(2)}) copy-start(bf16[12,64,576]{2,1,0:T(8,128)(2,1)} %param.18) | copy-start | bytes 2654212
  18.9 6.7 %copy-start.2 = (s32[192]{0:T(256)S(1)}, s32[192]{0:T(256)}, u32[]{:S(2)}) copy-start(s32[192]{0:T(256)} %param.19) | copy-start | bytes 2308
  18.9 7.6 %copy-start.7 = (bf16[16,64,576]{2,1,0:T(8,128)(2,1)S(1)}, bf16[16,64,576]{2,1,0:T(8,128)(2,1)}, u32[]{:S(2)}) copy-start(bf16[16,64,576]{2,1,0:T(8,128)(2,1)} %param.15) | copy-start | bytes 3538948
  18.9 7.6 %copy-start.8 = (s32[4]{0:T(128)S(1)}, s32[4]{0:T(128)}, u32[]{:S(2)}) copy-start(s32[4]{0:T(128)} %param.17) | copy-start | bytes 52
  18.9 65.4 %all-to-all-start = ((bf16[16,2,64,576]{3,2,1,0:T(8,128)(2,1)}), bf16[16,2,64,576]{3,2,1,0:T(8,128)(2,1)}, u32[]{:S(2)}, u32[]{:S(2)}) async-start(bf16[16,2,64,576]{3,2,1,0:T(8,128)(2,1)} %broadcast_select_fusion.1), calls=%async_computation | async-start | bytes 5242880 | tf_op jit(solution)/shard_map/all_to_all | solution.py:83
  25.5 119.7 %all-gather.2.cloned.1.call-start = ((), (), s32[]{:S(2)}) async-start(), calls=%async_computation.4 | async-start | bytes 4456448 | tf_op jit(solution)/shard_map/all_gather | solution.py:96
  87.4 0.7 copy-start.9
  89.8 6.2 %copy-start.4 = (s32[256,8]{0,1:T(8,128)S(1)}, s32[256,8]{0,1:T(8,128)}, u32[]{:S(2)}) copy-start(s32[256,8]{0,1:T(8,128)} %param.24) | copy-start | bytes 24580
  95.7 82.9 %all-reduce.2.cloned.1.call-start = ((), (), s32[]{:S(2)}) async-start(), calls=%async_computation.5 | async-start | bytes 917504 | tf_op jit(solution)/shard_map/psum | solution.py:115
  99.6 79.1 %copy-start.3 = (bf16[256,448]{0,1:T(8,128)(2,1)S(1)}, bf16[256,448]{0,1:T(8,128)(2,1)}, u32[]{:S(2)}) copy-start(bf16[256,448]{0,1:T(8,128)(2,1)} %param.23) | copy-start | bytes 688132
  196.5 6.7 %copy-start.5 = (bf16[7168]{0:T(1024)(128)(2,1)S(1)}, bf16[7168]{0:T(1024)(128)(2,1)}, u32[]{:S(2)}) copy-start(bf16[7168]{0:T(1024)(128)(2,1)} %param.26) | copy-start | bytes 43012
  196.5 76.6 %all-to-all-start.1 = ((bf16[16,192,448]{2,1,0:T(8,128)(2,1)}), bf16[16,192,448]{2,1,0:T(8,128)(2,1)}, u32[]{:S(2)}, u32[]{:S(2)}) async-start(bf16[16,192,448]{2,1,0:T(8,128)(2,1)} %broadcast_select_fusion), calls=%async_computation.1 | async-start | bytes 6291456 | tf_op jit(solution)/shard_map/all_to_all | solution.py:121
  203.1 139.0 %reduce-scatter.2.cloned.1.call-start = ((), (), s32[]{:S(2)}) async-start(), calls=%async_computation.6 | async-start | bytes 4128768 | tf_op jit(solution)/shard_map/reduce_scatter | solution.py:131
  390.9 11.0 %copy-start.6 = (f32[256,8]{0,1:T(8,128)S(1)}, f32[256,8]{0,1:T(8,128)}, u32[]{:S(2)}) copy-start(f32[256,8]{0,1:T(8,128)} %param.25) | copy-start | bytes 24580
  394.8 38.4 %all-to-all-start.2 = ((bf16[16,2,21504]{2,1,0:T(2,128)(2,1)}), bf16[16,2,21504]{2,1,0:T(2,128)(2,1)S(1)}, u32[]{:S(2)}, u32[]{:S(2)}) async-start(bf16[16,2,21504]{2,1,0:T(2,128)(2,1)} %reshape.370), calls=%async_computation.3 | async-start | bytes 2752512 | tf_op jit(solution)/shard_map/all_to_all | solution.py:134
  453.1 9.2 %copy-start.1 = (bf16[12,64,576]{2,1,0:T(8,128)(2,1)S(1)}, bf16[12,64,576]{2,1,0:T(8,128)(2,1)}, u32[]{:S(2)}) copy-start(bf16[12,64,576]{2,1,0:T(8,128)(2,1)} %param.18) | copy-start | bytes 2654212
Sparse Core Ops, SparseCore 0:
  95.9 49.3 all-gather.1
  152.6 26.0 all-reduce.1
  304.7 37.4 reduce-scatter.1
where the time goes:
time: 470 us; the launch traced here: 469 us
  waiting for transfers between devices  252 us (54%)
  local copies, waits for them, and re-layouts  72.9 us (16%)
  other arithmetic  72.3 us (15%)
  matrix products  38.2 us (8%)
  starting transfers between devices  20.1 us (4%)
  between operations  13.5 us (3%)
    all_to_all x1, waiting for transfers between devices, per_device(): lax.all_to_all(gathered, 'expert', split_axis=0, concat_axis=2, tiled=True)  69.9 us
    all_to_all x1, waiting for transfers between devices, per_device(): lax.all_to_all(outgoing, 'expert', split_axis=0, concat_axis=0, tiled=True)  49.6 us
    all_gather x1, waiting for transfers between devices, per_device(): lax.all_gather(attention, 'expert', axis=0, tiled=True)  45.6 us
    unnamed x1, other arithmetic  39.8 us
    reduce_scatter x1, waiting for transfers between devices, per_device(): lax.psum_scatter(partial_value.astype(jnp.bfloat16), 'head', scatter_dime...  37.6 us
    all_to_all x1, waiting for transfers between devices, per_device(): lax.all_to_all(shared.astype(jnp.bfloat16), 'expert', split_axis=2, conca...  31.1 us
    psum x1, waiting for transfers between devices, per_device(): summed = lax.psum(mixed, 'head')  18 us
    gather x1, local copies, waits for them, and re-layouts, per_device(): jnp.take(hidden_all, slot_rows, axis=0, mode='fill', fill_value=0)  13.2 us
  transfers between devices with their start and end apart: 6, of which 6 were waited for; matrix products, arithmetic and copies ran while one was open for 5% of the time, Pallas kernels for 0%

commit v1 on v0

--- a/solution.py
+++ b/solution.py
@@ -131,8 +131,14 @@
     shared = lax.psum_scatter(
         partial_value.astype(jnp.bfloat16), "head", scatter_dimension=1, tiled=True
     ).astype(jnp.float32)
-    returned = lax.all_to_all(
-        shared.astype(jnp.bfloat16), "expert", split_axis=2, concat_axis=0, tiled=True
+    returned = jnp.concatenate(
+        lax.all_to_all(
+            jnp.stack(jnp.split(shared.astype(jnp.bfloat16), lax.axis_size("expert"), axis=2)),
+            "expert",
+            0,
+            0,
+        ),
+        axis=0,
     ).astype(shared.dtype)
     ids_block = lax.dynamic_slice_in_dim(expert_ids, head_index * block_rows, block_rows)
     gates_block = lax.dynamic_slice_in_dim(expert_gates, head_index * block_rows, block_rows)

time: 470 us -> 429 us (0.913)
  other arithmetic: 72.3 us -> 27 us
    unnamed x1 -> x0, other arithmetic: 39.8 us -> none
    unnamed x27 -> x39, local copies, waits for them, and re-layouts: 12.6 us -> 24.8 us
    reduce_scatter x1 -> x0, local copies, waits for them, and re-layouts: 8.47 us -> none  [per_device(): lax.psum_scatter(partial_value.astype(jnp.bfloat16), 'head', scatter_dime...]
    convert_element_type x1, other arithmetic: 7.74 us -> 2.21 us  [per_device(): returned = jnp.concatenate(lax.all_to_all(jnp.stack(jnp.split(shared.asty...]
    convert_element_type x1 -> x0, local copies, waits for them, and re-layouts: 5.01 us -> none  [per_device(): returned = lax.all_to_all(shared.astype(jnp.bfloat16), 'expert', split_ax...]
where the time goes in v1:
time: 429 us; the launch traced here: 428 us
  waiting for transfers between devices  256 us (60%)
  local copies, waits for them, and re-layouts  73.2 us (17%)
  matrix products  38.2 us (9%)
  other arithmetic  27 us (6%)
  starting transfers between devices  20.3 us (5%)
  between operations  13.5 us (3%)
    all_to_all x1, waiting for transfers between devices, per_device(): lax.all_to_all(gathered, 'expert', split_axis=0, concat_axis=2, tiled=True)  69.6 us
    all_to_all x1, waiting for transfers between devices, per_device(): lax.all_to_all(outgoing, 'expert', split_axis=0, concat_axis=0, tiled=True)  49.6 us
    all_gather x1, waiting for transfers between devices, per_device(): lax.all_gather(attention, 'expert', axis=0, tiled=True)  45.6 us
    reduce_scatter x1, waiting for transfers between devices, per_device(): lax.psum_scatter(partial_value.astype(jnp.bfloat16), 'head', scatter_dime...  37.6 us
    all_to_all x1, waiting for transfers between devices, per_device(): lax.all_to_all(jnp.stack(jnp.split(shared.astype(jnp.bfloat16), lax.axis_...  35.3 us
    unnamed x39, local copies, waits for them, and re-layouts  24.8 us
    psum x1, waiting for transfers between devices, per_device(): summed = lax.psum(mixed, 'head')  18 us
    gather x1, local copies, waits for them, and re-layouts, per_device(): jnp.take(hidden_all, slot_rows, axis=0, mode='fill', fill_value=0)  13.2 us
  transfers between devices with their start and end apart: 6, of which 6 were waited for; matrix products, arithmetic and copies ran while one was open for 5% of the time, Pallas kernels for 0%

profile of v1, /device:TPU:13, one launch (start us, length us, event | category | flops | bytes accessed | tf_op | source)
XLA Modules:
  0.0 428.0 jit_solution(4008558633665412532)
XLA Ops:
  7.6 3.8 sort.17
  12.9 2.4 gather_fusion.1
  15.3 3.5 broadcast_select_fusion.1
  18.9 6.7 %all-to-all-start = ((bf16[16,2,64,576]{3,2,1,0:T(8,128)(2,1)}), bf16[16,2,64,576]{3,2,1,0:T(8,128)(2,1)}, u32[]{:S(2)}, u32[]{:S(2)}) async-start(bf16[16,2,64,576]{3,2,1,0:T(8,128)(2,1)} %broadcast_select_fusion.1), calls=%async_computation | async-start | bytes 5242880 | tf_op jit(solution)/shard_map/all_to_all | solution.py:83
  28.3 1.8 convolution_convert_fusion.3
  30.1 4.6 %fusion.28 = bf16[4,8192]{1,0:T(4,128)(2,1)S(1)} fusion(bf16[64,512,128]{2,1,0:T(8,128)(2,1)} %param.21, bf16[4,64,512]{2,1,0:T(8,128)(2,1)S(1)} %convolution_convert_fusion.3), kind=kOutput, calls=%fused_computation.44 | convolution fusion | flops 33587200 | bytes 8716288 | tf_op jit(solution)/shard_map/rhc,hcv->rhv/dot_general | solution.py:25
  34.7 49.6 %all-to-all-done = bf16[16,2,64,576]{3,2,1,0:T(8,128)(2,1)} async-done(((bf16[16,2,64,576]{3,2,1,0:T(8,128)(2,1)}), bf16[16,2,64,576]{3,2,1,0:T(8,128)(2,1)}, u32[]{:S(2)}, u32[]{:S(2)}) %all-to-all-start) | async-done | bytes 2359328 | tf_op jit(solution)/shard_map/all_to_all | solution.py:83
  84.3 2.5 gather_fusion.2
  89.8 4.8 %fusion.26 = bf16[12,64,128]{2,0,1:T(8,128)(2,1)S(1)} fusion(bf16[64,512,128]{2,1,0:T(8,128)(2,1)} %param.21, bf16[12,64,512]{2,1,0:T(8,128)(2,1)S(1)} %convolution_convert_fusion.1), kind=kOutput, calls=%fused_computation.40 | convolution fusion | flops 100761600 | bytes 9371648 | tf_op jit(solution)/shard_map/rhc,hcv->rhv/dot_general | solution.py:25
  96.3 2.8 select_reduce_fusion
  99.6 45.6 %all-gather.2.cloned.1.call-done = bf16[256,8192]{1,0:T(8,128)(2,1)} async-done(((bf16[16,8192]{1,0:T(8,128)(2,1)}), bf16[256,8192]{1,0:T(8,128)(2,1)}) %all-gather.2.cloned.1.call-update) | async-done | bytes 4194320 | tf_op jit(solution)/shard_map/all_gather | solution.py:96
  145.2 7.2 %fusion.75 = f32[256,448]{0,1:T(8,128)} fusion(bf16[256,8192]{1,0:T(8,128)(2,1)} %all-gather.2.cloned.1.call-done, bf16[8192,448]{0,1:T(8,128)(2,1)} %param.22), kind=kOutput, calls=%fused_computation.149 | convolution fusion | flops 1879048192 | bytes 11993088 | tf_op jit(solution)/shard_map/dot_general | solution.py:95
  152.5 8.1 %scatter_custom_fusion.1 = s32[3072]{0:T(1024)S(1)} fusion(s32[2048]{0:T(1024)S(1)} %bitcast.140, s32[2048]{0:T(1024)S(1)} %add_bitcast_fusion, s32[]{:T(128)} %constant.124.clone.1), kind=kCustom, calls=%fused_computation.115 | custom fusion | bytes 12292 | tf_op jit(solution)/shard_map/scatter | solution.py:113
  160.7 18.0 %all-reduce.2.cloned.1.call-done = f32[256,448]{0,1:T(8,128)} async-done(((f32[256,448]{0,1:T(8,128)}), f32[256,448]{0,1:T(8,128)}) %all-reduce.2.cloned.1.call-update) | async-done | bytes 458768 | tf_op jit(solution)/shard_map/psum | solution.py:115
  179.9 13.2 %gather_fusion.3 = bf16[3072,448]{1,0:T(8,128)(2,1)} fusion(bf16[256,448]{1,0:T(8,128)(2,1)S(1)} %copy.95, s32[3072]{0:T(1024)S(1)} %fusion.63), kind=kCustom, calls=%fused_computation.3 | custom fusion | bytes 5517312 | tf_op jit(solution)/shard_map/jit(_take)/gather | solution.py:118
  193.1 3.4 broadcast_select_fusion
  196.5 6.6 %all-to-all-start.1 = ((bf16[16,192,448]{2,1,0:T(8,128)(2,1)}), bf16[16,192,448]{2,1,0:T(8,128)(2,1)}, u32[]{:S(2)}, u32[]{:S(2)}) async-start(bf16[16,192,448]{2,1,0:T(8,128)(2,1)} %broadcast_select_fusion), calls=%async_computation.1 | async-start | bytes 6291456 | tf_op jit(solution)/shard_map/all_to_all | solution.py:121
  203.5 69.6 %all-to-all-done.1 = bf16[16,192,448]{2,1,0:T(8,128)(2,1)} async-done(((bf16[16,192,448]{2,1,0:T(8,128)(2,1)}), bf16[16,192,448]{2,1,0:T(8,128)(2,1)}, u32[]{:S(2)}, u32[]{:S(2)}) %all-to-all-start.1) | async-done | bytes 2752544 | tf_op jit(solution)/shard_map/all_to_all | solution.py:121
  273.1 2.7 fusion.8
  275.7 2.8 fusion.11
  278.5 3.4 copy.96
  282.0 6.4 %convert_element_type.116 = bf16[192,7168]{1,0:T(8,128)(2,1)} reshape(bf16[1,192,16,448]{3,2,1,0:T(8,128)(2,1)} %copy.96) | data formatting | bytes 5505024 | tf_op jit(solution)/shard_map/convert_element_type | solution.py:124
  288.3 5.5 %fusion.6 = f32[192,512]{1,0:T(8,128)S(1)} fusion(bf16[192,7168]{1,0:T(8,128)(2,1)} %convert_element_type.116, bf16[1,7168,512]{2,1,0:T(8,128)(2,1)} %param.27), kind=kOutput, calls=%fused_computation.16 | convolution fusion | flops 1409286144 | bytes 10485760 | tf_op jit(solution)/shard_map/esd,edf->esf/dot_general | solution.py:125
  293.8 10.7 %fusion.2 = bf16[1,192,7168]{2,1,0:T(8,128)(2,1)} fusion(bf16[1,512,7168]{2,1,0:T(8,128)(2,1)} %param.29, bf16[192,7168]{1,0:T(8,128)(2,1)} %convert_element_type.116, bf16[1,7168,512]{2,1,0:T(8,128)(2,1)} %param.28, f32[192,512]{1,0:T(8,128)S(1)} %fusion.6), kind=kOutput, calls=%fused_computation.10 | convolution fusion | flops 2820538368 | bytes 20578304 | tf_op jit(solution)/shard_map/esf,efd->esd/dot_general | solution.py:128
  304.5 37.6 %reduce-scatter.2.cloned.1.call-done = bf16[1,96,7168]{2,1,0:T(8,128)(2,1)} async-done(((bf16[1,192,7168]{2,1,0:T(8,128)(2,1)}), bf16[1,96,7168]{2,1,0:T(8,128)(2,1)}) %reduce-scatter.2.cloned.1.call-update) | async-done | bytes 1376272 | tf_op jit(solution)/shard_map/reduce_scatter | solution.py:131
  343.6 1.6 fusion.61
  346.8 1.6 fusion.59
  362.6 1.6 fusion.49
  367.4 6.5 %all-to-all-start.2 = ((bf16[16,1,96,448]{3,2,1,0:T(8,128)(2,1)}), bf16[16,1,96,448]{3,2,1,0:T(8,128)(2,1)S(1)}, u32[]{:S(2)}, u32[]{:S(2)}) async-start(bf16[16,1,96,448]{3,2,1,0:T(8,128)(2,1)} %fusion.47), calls=%async_computation.3 | async-start | bytes 3145728 | tf_op jit(solution)/shard_map/all_to_all | solution.py:135
  374.7 35.3 %all-to-all-done.2 = bf16[16,1,96,448]{3,2,1,0:T(8,128)(2,1)S(1)} async-done(((bf16[16,1,96,448]{3,2,1,0:T(8,128)(2,1)}), bf16[16,1,96,448]{3,2,1,0:T(8,128)(2,1)S(1)}, u32[]{:S(2)}, u32[]{:S(2)}) %all-to-all-start.2) | async-done | bytes 1376288 | tf_op jit(solution)/shard_map/all_to_all | solution.py:135
  410.1 2.2 bitcast_convert_fusion
  412.3 6.0 %gather_fusion.4 = f32[1024,448]{1,0:T(8,128)S(1)} fusion(f32[1536,448]{1,0:T(8,128)} %bitcast_convert_fusion, s32[1024]{0:T(1024)S(1)} %broadcast_clamp_fusion), kind=kCustom, calls=%fused_computation.4 | custom fusion | bytes 3674112 | tf_op jit(solution)/shard_map/jit(_take)/gather | solution.py:155
  (102 shorter events, 36.4 us)
Async XLA Ops:
  6.5 6.4 %copy-start = (bf16[12,64,576]{2,1,0:T(8,128)(2,1)S(1)}, bf16[12,64,576]{2,1,0:T(8,128)(2,1)}, u32[]{:S(2)}) copy-start(bf16[12,64,576]{2,1,0:T(8,128)(2,1)} %param.18) | copy-start | bytes 2654212
  18.9 6.7 %copy-start.2 = (s32[192]{0:T(256)S(1)}, s32[192]{0:T(256)}, u32[]{:S(2)}) copy-start(s32[192]{0:T(256)} %param.19) | copy-start | bytes 2308
  18.9 7.6 %copy-start.7 = (bf16[16,64,576]{2,1,0:T(8,128)(2,1)S(1)}, bf16[16,64,576]{2,1,0:T(8,128)(2,1)}, u32[]{:S(2)}) copy-start(bf16[16,64,576]{2,1,0:T(8,128)(2,1)} %param.15) | copy-start | bytes 3538948
  18.9 7.6 %copy-start.8 = (s32[4]{0:T(128)S(1)}, s32[4]{0:T(128)}, u32[]{:S(2)}) copy-start(s32[4]{0:T(128)} %param.17) | copy-start | bytes 52
  18.9 65.4 %all-to-all-start = ((bf16[16,2,64,576]{3,2,1,0:T(8,128)(2,1)}), bf16[16,2,64,576]{3,2,1,0:T(8,128)(2,1)}, u32[]{:S(2)}, u32[]{:S(2)}) async-start(bf16[16,2,64,576]{3,2,1,0:T(8,128)(2,1)} %broadcast_select_fusion.1), calls=%async_computation | async-start | bytes 5242880 | tf_op jit(solution)/shard_map/all_to_all | solution.py:83
  25.5 119.7 %all-gather.2.cloned.1.call-start = ((), (), s32[]{:S(2)}) async-start(), calls=%async_computation.4 | async-start | bytes 4456448 | tf_op jit(solution)/shard_map/all_gather | solution.py:96
  87.4 0.7 copy-start.9
  94.6 1.3 copy-start.4
  95.7 82.9 %all-reduce.2.cloned.1.call-start = ((), (), s32[]{:S(2)}) async-start(), calls=%async_computation.5 | async-start | bytes 917504 | tf_op jit(solution)/shard_map/psum | solution.py:115
  99.6 79.1 %copy-start.3 = (bf16[256,448]{0,1:T(8,128)(2,1)S(1)}, bf16[256,448]{0,1:T(8,128)(2,1)}, u32[]{:S(2)}) copy-start(bf16[256,448]{0,1:T(8,128)(2,1)} %param.23) | copy-start | bytes 688132
  196.5 6.9 %copy-start.5 = (bf16[7168]{0:T(1024)(128)(2,1)S(1)}, bf16[7168]{0:T(1024)(128)(2,1)}, u32[]{:S(2)}) copy-start(bf16[7168]{0:T(1024)(128)(2,1)} %param.26) | copy-start | bytes 43012
  196.5 76.6 %all-to-all-start.1 = ((bf16[16,192,448]{2,1,0:T(8,128)(2,1)}), bf16[16,192,448]{2,1,0:T(8,128)(2,1)}, u32[]{:S(2)}, u32[]{:S(2)}) async-start(bf16[16,192,448]{2,1,0:T(8,128)(2,1)} %broadcast_select_fusion), calls=%async_computation.1 | async-start | bytes 6291456 | tf_op jit(solution)/shard_map/all_to_all | solution.py:121
  203.1 139.0 %reduce-scatter.2.cloned.1.call-start = ((), (), s32[]{:S(2)}) async-start(), calls=%async_computation.6 | async-start | bytes 4128768 | tf_op jit(solution)/shard_map/reduce_scatter | solution.py:131
  362.6 12.0 %copy-start.6 = (f32[256,8]{0,1:T(8,128)S(1)}, f32[256,8]{0,1:T(8,128)}, u32[]{:S(2)}) copy-start(f32[256,8]{0,1:T(8,128)} %param.25) | copy-start | bytes 24580
  367.4 42.7 %all-to-all-start.2 = ((bf16[16,1,96,448]{3,2,1,0:T(8,128)(2,1)}), bf16[16,1,96,448]{3,2,1,0:T(8,128)(2,1)S(1)}, u32[]{:S(2)}, u32[]{:S(2)}) async-start(bf16[16,1,96,448]{3,2,1,0:T(8,128)(2,1)} %fusion.47), calls=%async_computation.3 | async-start | bytes 3145728 | tf_op jit(solution)/shard_map/all_to_all | solution.py:135
  412.3 9.2 %copy-start.1 = (bf16[12,64,576]{2,1,0:T(8,128)(2,1)S(1)}, bf16[12,64,576]{2,1,0:T(8,128)(2,1)}, u32[]{:S(2)}) copy-start(bf16[12,64,576]{2,1,0:T(8,128)(2,1)} %param.18) | copy-start | bytes 2654212
Sparse Core Ops, SparseCore 0:
  95.9 49.3 all-gather.1
  152.6 26.0 all-reduce.1
  304.7 37.4 reduce-scatter.1
